TPU v7x, 32 devices: a whole 2x2x4 slice. The times are simulated.
32 devices in a mesh: member: 8 (over z, x), space: 4 (over y, core).
Axes of the slice: x: 2, y: 2, z: 4, core: 2. Of those that a mesh axis runs over, the one named last changes fastest.
Arguments:
- alpha: float32 [16, 16, 32, 1280], P('member', None, 'space'), may hold values from -6 to 6
- perturb: bfloat16 [4, 16, 16, 32, 1280], P(None, 'member', None, 'space'), may hold values from -1.5 to 1.5
- kappa: float32 [32, 1280], P('space'), may hold values from 0.1 to 0.24
- land: int32 [32, 1280], P('space'), may hold values 0 or 1
- obs_weight: float32 [4, 16, 32, 1280], P(None, 'member', 'space'), may hold values from 0.2 to 5
- innovation: float32 [4, 16, 32, 1280], P(None, 'member', 'space'), may hold values from -6 to 6
Outputs:
- gradient: float32 [16, 16, 32, 1280], P('member', None, 'space')
- weighted_misfit: float32 [4, 16, 32, 1280], P(None, 'member', 'space')
All inputs are finite; a program needn't handle non-finite values. No bound on the sum of `land` on one device may be relied on, other than what follows from the above.
Results may differ from a plain program's by a relative error of at most 0.0003.
Values sent between devices are 32-bit elements; how exact they have to be, the bound alone decides.
No kernel may reach another device: no remote copies, remote signals or barrier semaphores. Data moves between devices by JAX's collectives and lax.ppermute only.
A program may use at most 64 MiB of HBM per device.

v0:
```python
import jax
import jax.numpy as jnp
from jax import lax
from jax.sharding import PartitionSpec as P

STEPS = 4


def extended_2(cells, sides, width):
    for axis, dim in sides:
        count = lax.axis_size(axis)
        ends = count - 1
        head = lax.slice_in_dim(cells, 0, width, axis=dim)
        tail = lax.slice_in_dim(cells, cells.shape[dim] - width, cells.shape[dim], axis=dim)
        cells = jnp.concatenate(
            [
                lax.ppermute(tail, axis, [(i, (i + 1) % count) for i in range(ends)]),
                cells,
                lax.ppermute(head, axis, [((i + 1) % count, i) for i in range(ends)]),
            ],
            axis=dim,
        )
    return cells


def smooth_step(padded, coef_east, coef_west, coef_north, coef_south):
    middle = padded[:, :, 1:-1, :]
    return (
        middle
        + coef_east * (jnp.roll(middle, -1, axis=-1) - middle)
        + coef_west * (jnp.roll(middle, 1, axis=-1) - middle)
        + coef_north * (padded[:, :, 2:, :] - middle)
        + coef_south * (padded[:, :, :-2, :] - middle)
    )


def body(alpha, perturb, kappa, land, obs_weight, innovation):
    tile_rows = alpha.shape[2]
    extended = extended_2(kappa, (("space", 0),), STEPS + 1)
    inner = extended[1:-1]
    coef_north = 0.5 * (inner + extended[2:])
    coef_south = 0.5 * (inner + extended[:-2])
    coef_east = 0.5 * (inner + jnp.roll(inner, -1, axis=1))
    coef_west = 0.5 * (inner + jnp.roll(inner, 1, axis=1))

    def diffuse(field):
        current = field
        for sweep in range(STEPS):
            padded = extended_2(current, (("space", 2),), 1)
            current = smooth_step(
                padded,
                coef_east[STEPS : STEPS + tile_rows],
                coef_west[STEPS : STEPS + tile_rows],
                coef_north[STEPS : STEPS + tile_rows],
                coef_south[STEPS : STEPS + tile_rows],
            )
        return current

    sea = land.astype(jnp.float32)
    local = diffuse(alpha) * sea
    partial_sum = jnp.sum(perturb * local[None], axis=1)
    total = lax.psum(partial_sum, "member")
    weight_all, innov_all = (
        lax.all_gather(obs_weight, "member", axis=1, tiled=True),
        lax.all_gather(innovation, "member", axis=1, tiled=True),
    )
    whole_misfit = weight_all * (total - innov_all)
    own_width = obs_weight.shape[1]
    weighted_misfit = lax.dynamic_slice_in_dim(
        whole_misfit, lax.axis_index("member") * own_width, own_width, 1
    )
    back = jnp.sum(perturb * whole_misfit[:, None], axis=0)
    gradient = diffuse(back * sea) + alpha
    return (gradient, weighted_misfit)


def solution(mesh):
    placed = (
        P("member", None, "space", None),
        P(None, "member", None, "space", None),
        P("space", None),
        P("space", None),
        P(None, "member", "space", None),
        P(None, "member", "space", None),
    )
    return jax.shard_map(
        body,
        mesh=mesh,
        in_specs=placed,
        out_specs=(P("member", None, "space", None), P(None, "member", "space", None)),
        check_vma=False,
    )
```

profile of v0, /device:TPU:1, one launch (start us, length us, event | category | flops | bytes accessed | tf_op | source)
XLA Modules:
  0.0 342.5 jit_solution(4764403704498449764)
XLA Ops:
  8.1 4.5 %collective-permute-start = (f32[5,1280]{1,0:T(8,128)S(1)}, f32[5,1280]{1,0:T(8,128)S(1)}, u32[]{:S(2)}, u32[]{:S(2)}) collective-permute-start(f32[5,1280]{1,0:T(8,128)S(1)} %get-tuple-element.61), channel_id=1, source_target_pairs={{0,1},{1,2},{2,3},{4,5},{5,6},{6,7},{8,9},{9,10},{10,11},{12,13},{... | collective-permute-start | bytes 76808 | tf_op jit(solution)/shard_map/ppermute | solution.py:17
  12.6 1.9 collective-permute-start.1
  14.6 2.1 fusion.113
  16.7 1.9 collective-permute-start.2
  18.7 3.8 %collective-permute-start.3 = (f32[2,16,1,1280]{3,1,2,0:T(8,128)S(1)}, f32[2,16,1,1280]{3,1,2,0:T(8,128)S(1)}, u32[]{:S(2)}, u32[]{:S(2)}) collective-permute-start(f32[2,16,1,1280]{3,1,2,0:T(8,128)S(1)} %copy.57), channel_id=1, source_target_pairs={{0,1},{1,2},{2,3},{4,5},{5,6},{6,7},{8,9},{9,10},{10,11},{12,13},{... | collective-permute-start | bytes 491528 | tf_op jit(solution)/shard_map/ppermute | solution.py:17
  23.5 1.2 collective-permute-done.3
  26.5 1.9 collective-permute-start.4
  28.5 4.4 %collective-permute-start.5 = (f32[2,16,1,1280]{3,1,2,0:T(8,128)S(1)}, f32[2,16,1,1280]{3,1,2,0:T(8,128)S(1)}, u32[]{:S(2)}, u32[]{:S(2)}) collective-permute-start(f32[2,16,1,1280]{3,1,2,0:T(8,128)S(1)} %copy.30), channel_id=1, source_target_pairs={{0,1},{1,2},{2,3},{4,5},{5,6},{6,7},{8,9},{9,10},{10,11},{12,13},{... | collective-permute-start | bytes 491528 | tf_op jit(solution)/shard_map/ppermute | solution.py:17
  34.1 1.0 collective-permute-done.5
  37.0 1.9 collective-permute-start.6
  38.9 4.4 %collective-permute-start.7 = (f32[2,16,1,1280]{3,1,2,0:T(8,128)S(1)}, f32[2,16,1,1280]{3,1,2,0:T(8,128)S(1)}, u32[]{:S(2)}, u32[]{:S(2)}) collective-permute-start(f32[2,16,1,1280]{3,1,2,0:T(8,128)S(1)} %copy.34), channel_id=1, source_target_pairs={{0,1},{1,2},{2,3},{4,5},{5,6},{6,7},{8,9},{9,10},{10,11},{12,13},{... | collective-permute-start | bytes 491528 | tf_op jit(solution)/shard_map/ppermute | solution.py:17
  44.5 1.0 collective-permute-done.7
  47.4 1.9 collective-permute-start.8
  49.4 4.4 %collective-permute-start.9 = (f32[2,16,1,1280]{3,1,2,0:T(8,128)S(1)}, f32[2,16,1,1280]{3,1,2,0:T(8,128)S(1)}, u32[]{:S(2)}, u32[]{:S(2)}) collective-permute-start(f32[2,16,1,1280]{3,1,2,0:T(8,128)S(1)} %copy.38), channel_id=1, source_target_pairs={{0,1},{1,2},{2,3},{4,5},{5,6},{6,7},{8,9},{9,10},{10,11},{12,13},{... | collective-permute-start | bytes 491528 | tf_op jit(solution)/shard_map/ppermute | solution.py:17
  55.0 1.0 collective-permute-done.9
  56.2 1.1 fusion.30
  57.9 2.1 fusion
  61.6 115.5 %all-reduce.2.cloned.1.call-done = f32[4,16,8,1280]{3,2,1,0:T(8,128)} async-done(((f32[4,16,8,1280]{3,2,1,0:T(8,128)}), f32[4,16,8,1280]{3,2,1,0:T(8,128)}) %all-reduce.2.cloned.1.call-update) | async-done | bytes 2621456 | tf_op jit(solution)/shard_map/psum | solution.py:62
  177.0 55.2 %all-gather.3.cloned.1.call-done = f32[4,16,8,1280]{3,2,1,0:T(8,128)} async-done(((f32[4,2,8,1280]{3,2,1,0:T(8,128)}), f32[4,16,8,1280]{3,2,1,0:T(8,128)}) %all-gather.3.cloned.1.call-update) | async-done | bytes 2621456 | tf_op jit(solution)/shard_map/all_gather | solution.py:64
  232.2 55.2 %all-gather.5.cloned.1.call-done = f32[4,16,8,1280]{3,2,1,0:T(8,128)} async-done(((f32[4,2,8,1280]{3,2,1,0:T(8,128)}), f32[4,16,8,1280]{3,2,1,0:T(8,128)}) %all-gather.5.cloned.1.call-update) | async-done | bytes 2621456 | tf_op jit(solution)/shard_map/all_gather | solution.py:65
  287.5 3.9 %subtract_multiply_fusion = f32[4,16,8,1280]{3,2,1,0:T(8,128)S(1)} fusion(f32[4,16,8,1280]{3,2,1,0:T(8,128)} %all-gather.3.cloned.1.call-done, f32[4,16,8,1280]{3,2,1,0:T(8,128)} %all-reduce.2.cloned.1.call-done, f32[4,16,8,1280]{3,2,1,0:T(8,128)} %all-gather.5.cloned.1.call-done), kind=kLoop, calls=%fused_computation.4 | loop fusion | flops 1310720 | bytes 10485760 | tf_op jit(solution)/shard_map/mul | solution.py:67
  292.8 4.2 %collective-permute-start.10 = (f32[2,16,1,1280]{3,1,2,0:T(8,128)S(1)}, f32[2,16,1,1280]{3,1,2,0:T(8,128)S(1)}, u32[]{:S(2)}, u32[]{:S(2)}) collective-permute-start(f32[2,16,1,1280]{3,1,2,0:T(8,128)S(1)} %copy.40), channel_id=1, source_target_pairs={{1,0},{2,1},{3,2},{5,4},{6,5},{7,6},{9,8},{10,9},{11,10},{13,12},{... | collective-permute-start | bytes 491528 | tf_op jit(solution)/shard_map/ppermute | solution.py:19
  297.0 3.0 collective-permute-start.11
  304.1 1.9 collective-permute-start.12
  306.1 4.4 %collective-permute-start.13 = (f32[2,16,1,1280]{3,1,2,0:T(8,128)S(1)}, f32[2,16,1,1280]{3,1,2,0:T(8,128)S(1)}, u32[]{:S(2)}, u32[]{:S(2)}) collective-permute-start(f32[2,16,1,1280]{3,1,2,0:T(8,128)S(1)} %copy.46), channel_id=1, source_target_pairs={{0,1},{1,2},{2,3},{4,5},{5,6},{6,7},{8,9},{9,10},{10,11},{12,13},{... | collective-permute-start | bytes 491528 | tf_op jit(solution)/shard_map/ppermute | solution.py:17
  311.7 1.0 collective-permute-done.13
  314.6 1.9 collective-permute-start.14
  316.5 4.4 %collective-permute-start.15 = (f32[2,16,1,1280]{3,1,2,0:T(8,128)S(1)}, f32[2,16,1,1280]{3,1,2,0:T(8,128)S(1)}, u32[]{:S(2)}, u32[]{:S(2)}) collective-permute-start(f32[2,16,1,1280]{3,1,2,0:T(8,128)S(1)} %copy.50), channel_id=1, source_target_pairs={{0,1},{1,2},{2,3},{4,5},{5,6},{6,7},{8,9},{9,10},{10,11},{12,13},{... | collective-permute-start | bytes 491528 | tf_op jit(solution)/shard_map/ppermute | solution.py:17
  323.3 1.1 fusion.11
  325.1 1.9 collective-permute-start.16
  327.0 4.4 %collective-permute-start.17 = (f32[2,16,1,1280]{3,1,2,0:T(8,128)S(1)}, f32[2,16,1,1280]{3,1,2,0:T(8,128)S(1)}, u32[]{:S(2)}, u32[]{:S(2)}) collective-permute-start(f32[2,16,1,1280]{3,1,2,0:T(8,128)S(1)} %copy.54), channel_id=1, source_target_pairs={{0,1},{1,2},{2,3},{4,5},{5,6},{6,7},{8,9},{9,10},{10,11},{12,13},{... | collective-permute-start | bytes 491528 | tf_op jit(solution)/shard_map/ppermute | solution.py:17
  333.8 2.2 fusion.5
  (98 shorter events, 27.4 us)
Async XLA Ops:
  7.2 15.3 %copy-start = (f32[2,16,8,1280]{3,2,1,0:T(8,128)S(1)}, f32[2,16,8,1280]{3,2,1,0:T(8,128)}, u32[]{:S(2)}) copy-start(f32[2,16,8,1280]{3,2,1,0:T(8,128)} %param.6) | copy-start | bytes 3932164
  7.2 169.9 %all-reduce.2.cloned.1.call-start = ((), (), s32[]{:S(2)}) async-start(), calls=%async_computation.1 | async-start | bytes 5242880 | tf_op jit(solution)/shard_map/psum | solution.py:62
  8.1 14.9 %collective-permute-start = (f32[5,1280]{1,0:T(8,128)S(1)}, f32[5,1280]{1,0:T(8,128)S(1)}, u32[]{:S(2)}, u32[]{:S(2)}) collective-permute-start(f32[5,1280]{1,0:T(8,128)S(1)} %get-tuple-element.61), channel_id=1, source_target_pairs={{0,1},{1,2},{2,3},{4,5},{5,6},{6,7},{8,9},{9,10},{10,11},{12,13},{... | collective-permute-start | bytes 76808 | tf_op jit(solution)/shard_map/ppermute | solution.py:17
  12.6 10.4 %collective-permute-start.1 = (f32[5,1280]{1,0:T(8,128)S(1)}, f32[5,1280]{1,0:T(8,128)S(1)}, u32[]{:S(2)}, u32[]{:S(2)}) collective-permute-start(f32[5,1280]{1,0:T(8,128)S(1)} %get-tuple-element.62), channel_id=1, source_target_pairs={{1,0},{2,1},{3,2},{5,4},{6,5},{7,6},{9,8},{10,9},{11,10},{13,12},{... | collective-permute-start | bytes 76808 | tf_op jit(solution)/shard_map/ppermute | solution.py:19
  16.7 6.6 %collective-permute-start.2 = (f32[2,16,1,1280]{3,1,2,0:T(8,128)S(1)}, f32[2,16,1,1280]{3,1,2,0:T(8,128)S(1)}, u32[]{:S(2)}, u32[]{:S(2)}) collective-permute-start(f32[2,16,1,1280]{3,1,2,0:T(8,128)S(1)} %copy.56), channel_id=1, source_target_pairs={{1,0},{2,1},{3,2},{5,4},{6,5},{7,6},{9,8},{10,9},{11,10},{13,12},{... | collective-permute-start | bytes 491528 | tf_op jit(solution)/shard_map/ppermute | solution.py:19
  18.6 4.3 %copy-start.4 = (s32[8,1280]{1,0:T(8,128)S(1)}, s32[8,1280]{1,0:T(8,128)}, u32[]{:S(2)}) copy-start(s32[8,1280]{1,0:T(8,128)} %param.9) | copy-start | bytes 122884
  18.6 4.4 %copy-start.3 = (f32[8,1280]{1,0:T(8,128)S(1)}, f32[8,1280]{1,0:T(8,128)}, u32[]{:S(2)}) copy-start(f32[8,1280]{1,0:T(8,128)} %param.8) | copy-start | bytes 122884
  18.7 6.0 %collective-permute-start.3 = (f32[2,16,1,1280]{3,1,2,0:T(8,128)S(1)}, f32[2,16,1,1280]{3,1,2,0:T(8,128)S(1)}, u32[]{:S(2)}, u32[]{:S(2)}) collective-permute-start(f32[2,16,1,1280]{3,1,2,0:T(8,128)S(1)} %copy.57), channel_id=1, source_target_pairs={{0,1},{1,2},{2,3},{4,5},{5,6},{6,7},{8,9},{9,10},{10,11},{12,13},{... | collective-permute-start | bytes 491528 | tf_op jit(solution)/shard_map/ppermute | solution.py:17
  26.5 7.4 %collective-permute-start.4 = (f32[2,16,1,1280]{3,1,2,0:T(8,128)S(1)}, f32[2,16,1,1280]{3,1,2,0:T(8,128)S(1)}, u32[]{:S(2)}, u32[]{:S(2)}) collective-permute-start(f32[2,16,1,1280]{3,1,2,0:T(8,128)S(1)} %copy.28), channel_id=1, source_target_pairs={{1,0},{2,1},{3,2},{5,4},{6,5},{7,6},{9,8},{10,9},{11,10},{13,12},{... | collective-permute-start | bytes 491528 | tf_op jit(solution)/shard_map/ppermute | solution.py:19
  28.5 6.6 %collective-permute-start.5 = (f32[2,16,1,1280]{3,1,2,0:T(8,128)S(1)}, f32[2,16,1,1280]{3,1,2,0:T(8,128)S(1)}, u32[]{:S(2)}, u32[]{:S(2)}) collective-permute-start(f32[2,16,1,1280]{3,1,2,0:T(8,128)S(1)} %copy.30), channel_id=1, source_target_pairs={{0,1},{1,2},{2,3},{4,5},{5,6},{6,7},{8,9},{9,10},{10,11},{12,13},{... | collective-permute-start | bytes 491528 | tf_op jit(solution)/shard_map/ppermute | solution.py:17
  37.0 7.4 %collective-permute-start.6 = (f32[2,16,1,1280]{3,1,2,0:T(8,128)S(1)}, f32[2,16,1,1280]{3,1,2,0:T(8,128)S(1)}, u32[]{:S(2)}, u32[]{:S(2)}) collective-permute-start(f32[2,16,1,1280]{3,1,2,0:T(8,128)S(1)} %copy.32), channel_id=1, source_target_pairs={{1,0},{2,1},{3,2},{5,4},{6,5},{7,6},{9,8},{10,9},{11,10},{13,12},{... | collective-permute-start | bytes 491528 | tf_op jit(solution)/shard_map/ppermute | solution.py:19
  38.9 6.6 %collective-permute-start.7 = (f32[2,16,1,1280]{3,1,2,0:T(8,128)S(1)}, f32[2,16,1,1280]{3,1,2,0:T(8,128)S(1)}, u32[]{:S(2)}, u32[]{:S(2)}) collective-permute-start(f32[2,16,1,1280]{3,1,2,0:T(8,128)S(1)} %copy.34), channel_id=1, source_target_pairs={{0,1},{1,2},{2,3},{4,5},{5,6},{6,7},{8,9},{9,10},{10,11},{12,13},{... | collective-permute-start | bytes 491528 | tf_op jit(solution)/shard_map/ppermute | solution.py:17
  47.4 7.4 %collective-permute-start.8 = (f32[2,16,1,1280]{3,1,2,0:T(8,128)S(1)}, f32[2,16,1,1280]{3,1,2,0:T(8,128)S(1)}, u32[]{:S(2)}, u32[]{:S(2)}) collective-permute-start(f32[2,16,1,1280]{3,1,2,0:T(8,128)S(1)} %copy.36), channel_id=1, source_target_pairs={{1,0},{2,1},{3,2},{5,4},{6,5},{7,6},{9,8},{10,9},{11,10},{13,12},{... | collective-permute-start | bytes 491528 | tf_op jit(solution)/shard_map/ppermute | solution.py:19
  49.4 6.6 %collective-permute-start.9 = (f32[2,16,1,1280]{3,1,2,0:T(8,128)S(1)}, f32[2,16,1,1280]{3,1,2,0:T(8,128)S(1)}, u32[]{:S(2)}, u32[]{:S(2)}) collective-permute-start(f32[2,16,1,1280]{3,1,2,0:T(8,128)S(1)} %copy.38), channel_id=1, source_target_pairs={{0,1},{1,2},{2,3},{4,5},{5,6},{6,7},{8,9},{9,10},{10,11},{12,13},{... | collective-permute-start | bytes 491528 | tf_op jit(solution)/shard_map/ppermute | solution.py:17
  56.2 1.7 copy-start.1
  60.1 172.1 %all-gather.3.cloned.1.call-start = ((), (), s32[]{:S(2)}) async-start(), calls=%async_computation | async-start | bytes 2949120 | tf_op jit(solution)/shard_map/all_gather | solution.py:64
  60.9 226.6 %all-gather.5.cloned.1.call-start = ((), (), s32[]{:S(2)}) async-start(), calls=%async_computation.2 | async-start | bytes 2949120 | tf_op jit(solution)/shard_map/all_gather | solution.py:65
  287.5 4.0 %copy-start.2 = (bf16[4,2,16,8,1280]{4,3,2,1,0:T(8,128)(2,1)S(1)}, bf16[4,2,16,8,1280]{4,3,2,1,0:T(8,128)(2,1)}, u32[]{:S(2)}) copy-start(bf16[4,2,16,8,1280]{4,3,2,1,0:T(8,128)(2,1)} %param.7) | copy-start | bytes 7864324
  292.8 8.2 %collective-permute-start.10 = (f32[2,16,1,1280]{3,1,2,0:T(8,128)S(1)}, f32[2,16,1,1280]{3,1,2,0:T(8,128)S(1)}, u32[]{:S(2)}, u32[]{:S(2)}) collective-permute-start(f32[2,16,1,1280]{3,1,2,0:T(8,128)S(1)} %copy.40), channel_id=1, source_target_pairs={{1,0},{2,1},{3,2},{5,4},{6,5},{7,6},{9,8},{10,9},{11,10},{13,12},{... | collective-permute-start | bytes 491528 | tf_op jit(solution)/shard_map/ppermute | solution.py:19
  297.0 5.2 %collective-permute-start.11 = (f32[2,16,1,1280]{3,1,2,0:T(8,128)S(1)}, f32[2,16,1,1280]{3,1,2,0:T(8,128)S(1)}, u32[]{:S(2)}, u32[]{:S(2)}) collective-permute-start(f32[2,16,1,1280]{3,1,2,0:T(8,128)S(1)} %copy.42), channel_id=1, source_target_pairs={{0,1},{1,2},{2,3},{4,5},{5,6},{6,7},{8,9},{9,10},{10,11},{12,13},{... | collective-permute-start | bytes 491528 | tf_op jit(solution)/shard_map/ppermute | solution.py:17
  304.1 7.4 %collective-permute-start.12 = (f32[2,16,1,1280]{3,1,2,0:T(8,128)S(1)}, f32[2,16,1,1280]{3,1,2,0:T(8,128)S(1)}, u32[]{:S(2)}, u32[]{:S(2)}) collective-permute-start(f32[2,16,1,1280]{3,1,2,0:T(8,128)S(1)} %copy.44), channel_id=1, source_target_pairs={{1,0},{2,1},{3,2},{5,4},{6,5},{7,6},{9,8},{10,9},{11,10},{13,12},{... | collective-permute-start | bytes 491528 | tf_op jit(solution)/shard_map/ppermute | solution.py:19
  306.1 6.6 %collective-permute-start.13 = (f32[2,16,1,1280]{3,1,2,0:T(8,128)S(1)}, f32[2,16,1,1280]{3,1,2,0:T(8,128)S(1)}, u32[]{:S(2)}, u32[]{:S(2)}) collective-permute-start(f32[2,16,1,1280]{3,1,2,0:T(8,128)S(1)} %copy.46), channel_id=1, source_target_pairs={{0,1},{1,2},{2,3},{4,5},{5,6},{6,7},{8,9},{9,10},{10,11},{12,13},{... | collective-permute-start | bytes 491528 | tf_op jit(solution)/shard_map/ppermute | solution.py:17
  314.6 7.4 %collective-permute-start.14 = (f32[2,16,1,1280]{3,1,2,0:T(8,128)S(1)}, f32[2,16,1,1280]{3,1,2,0:T(8,128)S(1)}, u32[]{:S(2)}, u32[]{:S(2)}) collective-permute-start(f32[2,16,1,1280]{3,1,2,0:T(8,128)S(1)} %copy.48), channel_id=1, source_target_pairs={{1,0},{2,1},{3,2},{5,4},{6,5},{7,6},{9,8},{10,9},{11,10},{13,12},{... | collective-permute-start | bytes 491528 | tf_op jit(solution)/shard_map/ppermute | solution.py:19
  316.5 6.6 %collective-permute-start.15 = (f32[2,16,1,1280]{3,1,2,0:T(8,128)S(1)}, f32[2,16,1,1280]{3,1,2,0:T(8,128)S(1)}, u32[]{:S(2)}, u32[]{:S(2)}) collective-permute-start(f32[2,16,1,1280]{3,1,2,0:T(8,128)S(1)} %copy.50), channel_id=1, source_target_pairs={{0,1},{1,2},{2,3},{4,5},{5,6},{6,7},{8,9},{9,10},{10,11},{12,13},{... | collective-permute-start | bytes 491528 | tf_op jit(solution)/shard_map/ppermute | solution.py:17
  325.1 7.4 %collective-permute-start.16 = (f32[2,16,1,1280]{3,1,2,0:T(8,128)S(1)}, f32[2,16,1,1280]{3,1,2,0:T(8,128)S(1)}, u32[]{:S(2)}, u32[]{:S(2)}) collective-permute-start(f32[2,16,1,1280]{3,1,2,0:T(8,128)S(1)} %copy.52), channel_id=1, source_target_pairs={{1,0},{2,1},{3,2},{5,4},{6,5},{7,6},{9,8},{10,9},{11,10},{13,12},{... | collective-permute-start | bytes 491528 | tf_op jit(solution)/shard_map/ppermute | solution.py:19
  327.0 6.6 %collective-permute-start.17 = (f32[2,16,1,1280]{3,1,2,0:T(8,128)S(1)}, f32[2,16,1,1280]{3,1,2,0:T(8,128)S(1)}, u32[]{:S(2)}, u32[]{:S(2)}) collective-permute-start(f32[2,16,1,1280]{3,1,2,0:T(8,128)S(1)} %copy.54), channel_id=1, source_target_pairs={{0,1},{1,2},{2,3},{4,5},{5,6},{6,7},{8,9},{9,10},{10,11},{12,13},{... | collective-permute-start | bytes 491528 | tf_op jit(solution)/shard_map/ppermute | solution.py:17
Sparse Core Ops, SparseCore 0:
  60.2 116.7 all-reduce.1
  179.2 52.9 all-gather.2
  234.4 52.9 all-gather.4
where the time goes:
time: 343 us
  waiting for transfers between devices  241 us (70%)
  starting transfers between devices  57.5 us (17%)
  other arithmetic  16.3 us (5%)
  between operations  14.4 us (4%)
  local copies, waits for them, and re-layouts  13.1 us (4%)
    psum x1, waiting for transfers between devices, body(): total = lax.psum(partial_sum, 'member')  115 us
    all_gather x1, waiting for transfers between devices, body(): lax.all_gather(innovation, 'member', axis=1, tiled=True)  55.2 us
    all_gather x1, waiting for transfers between devices, body(): lax.all_gather(obs_weight, 'member', axis=1, tiled=True)  55.2 us
    ppermute x9, starting transfers between devices, extended_2(): lax.ppermute(tail, axis, [(i, (i + 1) % count) for i in range(ends)])  37.6 us
    ppermute x9, starting transfers between devices, extended_2(): lax.ppermute(head, axis, [((i + 1) % count, i) for i in range(ends)])  19.5 us
    ppermute x9, waiting for transfers between devices, extended_2(): lax.ppermute(tail, axis, [(i, (i + 1) % count) for i in range(ends)])  8.39 us
  transfers between devices with their start and end apart: 21, of which 19 were waited for; matrix products, arithmetic and copies ran while one was open for 2% of the time, Pallas kernels for 0%

commit v1 on v0

--- a/solution.py
+++ b/solution.py
@@ -59,7 +59,8 @@
     sea = land.astype(jnp.float32)
     local = diffuse(alpha) * sea
     partial_sum = jnp.sum(perturb * local[None], axis=1)
-    total = lax.psum(partial_sum, "member")
+    pieces = lax.all_gather(partial_sum, "member")
+    total = jnp.sum(pieces, axis=0)
     weight_all, innov_all = (
         lax.all_gather(obs_weight, "member", axis=1, tiled=True),
         lax.all_gather(innovation, "member", axis=1, tiled=True),

time: 343 us -> 630 us (1.84)
  waiting for transfers between devices: 241 us -> 518 us
  other arithmetic: 16.3 us -> 25.9 us
    all_gather x0 -> x1, waiting for transfers between devices: none -> 402 us  [body(): pieces = lax.all_gather(partial_sum, 'member')]
    psum x1 -> x0, waiting for transfers between devices: 115 us -> none  [body(): total = lax.psum(partial_sum, 'member')]
    all_gather x1, waiting for transfers between devices: 55.2 us -> 45.5 us  [body(): lax.all_gather(obs_weight, 'member', axis=1, tiled=True)]
    reduce_sum x0 -> x1, other arithmetic: none -> 9.65 us  [body(): total = jnp.sum(pieces, axis=0)]
where the time goes in v1:
time: 630 us; the launch traced here: 629 us
  waiting for transfers between devices  518 us (82%)
  starting transfers between devices  57.5 us (9%)
  other arithmetic  25.9 us (4%)
  between operations  14.4 us (2%)
  local copies, waits for them, and re-layouts  12.9 us (2%)
    all_gather x1, waiting for transfers between devices, body(): pieces = lax.all_gather(partial_sum, 'member')  402 us
    all_gather x1, waiting for transfers between devices, body(): lax.all_gather(innovation, 'member', axis=1, tiled=True)  55.2 us
    all_gather x1, waiting for transfers between devices, body(): lax.all_gather(obs_weight, 'member', axis=1, tiled=True)  45.5 us
    ppermute x9, starting transfers between devices, extended_2(): lax.ppermute(tail, axis, [(i, (i + 1) % count) for i in range(ends)])  37.6 us
    ppermute x9, starting transfers between devices, extended_2(): lax.ppermute(head, axis, [((i + 1) % count, i) for i in range(ends)])  19.5 us
  transfers between devices with their start and end apart: 21, of which 19 were waited for; matrix products, arithmetic and copies ran while one was open for 2% of the time, Pallas kernels for 0%

profile of v1, /device:TPU:1, one launch (start us, length us, event | category | flops | bytes accessed | tf_op | source)
XLA Modules:
  0.0 629.0 jit_solution(3636558020668795434)
XLA Ops:
  8.1 4.5 collective-permute-start
  12.6 1.9 collective-permute-start.1
  14.6 1.9 fusion.113
  16.5 1.9 collective-permute-start.2
  18.5 3.8 collective-permute-start.3
  23.3 1.2 collective-permute-done.3
  26.4 1.9 collective-permute-start.4
  28.3 4.4 collective-permute-start.5
  36.8 1.9 collective-permute-start.6
  38.8 4.4 collective-permute-start.7
  44.4 1.0 collective-permute-done.7
  47.3 1.9 collective-permute-start.8
  49.2 4.4 collective-permute-start.9
  56.0 1.1 fusion.30
  57.8 2.1 fusion
  61.4 402.1 %all-gather.9.cloned.1.call-done = f32[32,16,8,1280]{3,2,1,0:T(8,128)} async-done(((f32[4,16,8,1280]{3,2,1,0:T(8,128)}), f32[32,16,8,1280]{3,2,1,0:T(8,128)}) %all-gather.9.cloned.1.call-update) | async-done | bytes 20971536 | tf_op jit(solution)/shard_map/all_gather | solution.py:62
  463.5 9.7 %reduce_sum.28 = f32[4,16,8,1280]{3,2,1,0:T(8,128)} reduce(f32[8,4,16,8,1280]{4,3,2,1,0:T(8,128)} %bitcast.1, f32[]{:T(128)} %constant.3.clone.1), dimensions={0}, to_apply=%region_1.2 | reduce | flops 4587520 | bytes 23592964 | tf_op jit(solution)/shard_map/reduce_sum | solution.py:63
  473.2 45.5 %all-gather.5.cloned.1.call-done = f32[4,16,8,1280]{3,2,1,0:T(8,128)} async-done(((f32[4,2,8,1280]{3,2,1,0:T(8,128)}), f32[4,16,8,1280]{3,2,1,0:T(8,128)}) %all-gather.5.cloned.1.call-update) | async-done | bytes 2621456 | tf_op jit(solution)/shard_map/all_gather | solution.py:65
  518.7 55.2 %all-gather.7.cloned.1.call-done = f32[4,16,8,1280]{3,2,1,0:T(8,128)} async-done(((f32[4,2,8,1280]{3,2,1,0:T(8,128)}), f32[4,16,8,1280]{3,2,1,0:T(8,128)}) %all-gather.7.cloned.1.call-update) | async-done | bytes 2621456 | tf_op jit(solution)/shard_map/all_gather | solution.py:66
  573.9 3.9 subtract_multiply_fusion
  579.3 4.2 collective-permute-start.10
  583.5 3.0 collective-permute-start.11
  587.7 1.0 collective-permute-done.11
  590.6 1.9 collective-permute-start.12
  592.5 4.4 collective-permute-start.13
  598.1 1.0 collective-permute-done.13
  601.0 1.9 collective-permute-start.14
  603.0 4.4 collective-permute-start.15
  609.8 1.1 fusion.11
  611.5 1.9 collective-permute-start.16
  613.5 4.4 collective-permute-start.17
  620.3 2.2 fusion.5
  (99 shorter events, 28.4 us)
Async XLA Ops:
  7.2 15.1 %copy-start = (f32[2,16,8,1280]{3,2,1,0:T(8,128)S(1)}, f32[2,16,8,1280]{3,2,1,0:T(8,128)}, u32[]{:S(2)}) copy-start(f32[2,16,8,1280]{3,2,1,0:T(8,128)} %param.6) | copy-start | bytes 3932164
  7.2 456.3 %all-gather.9.cloned.1.call-start = ((), (), s32[]{:S(2)}) async-start(), calls=%async_computation.2 | async-start | bytes 23592960 | tf_op jit(solution)/shard_map/all_gather | solution.py:62
  8.1 14.7 %collective-permute-start = (f32[5,1280]{1,0:T(8,128)S(1)}, f32[5,1280]{1,0:T(8,128)S(1)}, u32[]{:S(2)}, u32[]{:S(2)}) collective-permute-start(f32[5,1280]{1,0:T(8,128)S(1)} %get-tuple-element.61), channel_id=1, source_target_pairs={{0,1},{1,2},{2,3},{4,5},{5,6},{6,7},{8,9},{9,10},{10,11},{12,13},{... | collective-permute-start | bytes 76808 | tf_op jit(solution)/shard_map/ppermute | solution.py:17
  12.6 10.2 %collective-permute-start.1 = (f32[5,1280]{1,0:T(8,128)S(1)}, f32[5,1280]{1,0:T(8,128)S(1)}, u32[]{:S(2)}, u32[]{:S(2)}) collective-permute-start(f32[5,1280]{1,0:T(8,128)S(1)} %get-tuple-element.62), channel_id=1, source_target_pairs={{1,0},{2,1},{3,2},{5,4},{6,5},{7,6},{9,8},{10,9},{11,10},{13,12},{... | collective-permute-start | bytes 76808 | tf_op jit(solution)/shard_map/ppermute | solution.py:19
  16.5 6.6 %collective-permute-start.2 = (f32[2,16,1,1280]{3,1,2,0:T(8,128)S(1)}, f32[2,16,1,1280]{3,1,2,0:T(8,128)S(1)}, u32[]{:S(2)}, u32[]{:S(2)}) collective-permute-start(f32[2,16,1,1280]{3,1,2,0:T(8,128)S(1)} %copy.56), channel_id=1, source_target_pairs={{1,0},{2,1},{3,2},{5,4},{6,5},{7,6},{9,8},{10,9},{11,10},{13,12},{... | collective-permute-start | bytes 491528 | tf_op jit(solution)/shard_map/ppermute | solution.py:19
  18.5 4.3 copy-start.4
  18.5 4.4 copy-start.3
  18.5 6.0 collective-permute-start.3
  26.4 7.4 %collective-permute-start.4 = (f32[2,16,1,1280]{3,1,2,0:T(8,128)S(1)}, f32[2,16,1,1280]{3,1,2,0:T(8,128)S(1)}, u32[]{:S(2)}, u32[]{:S(2)}) collective-permute-start(f32[2,16,1,1280]{3,1,2,0:T(8,128)S(1)} %copy.28), channel_id=1, source_target_pairs={{1,0},{2,1},{3,2},{5,4},{6,5},{7,6},{9,8},{10,9},{11,10},{13,12},{... | collective-permute-start | bytes 491528 | tf_op jit(solution)/shard_map/ppermute | solution.py:19
  28.3 6.6 %collective-permute-start.5 = (f32[2,16,1,1280]{3,1,2,0:T(8,128)S(1)}, f32[2,16,1,1280]{3,1,2,0:T(8,128)S(1)}, u32[]{:S(2)}, u32[]{:S(2)}) collective-permute-start(f32[2,16,1,1280]{3,1,2,0:T(8,128)S(1)} %copy.30), channel_id=1, source_target_pairs={{0,1},{1,2},{2,3},{4,5},{5,6},{6,7},{8,9},{9,10},{10,11},{12,13},{... | collective-permute-start | bytes 491528 | tf_op jit(solution)/shard_map/ppermute | solution.py:17
  36.8 7.4 %collective-permute-start.6 = (f32[2,16,1,1280]{3,1,2,0:T(8,128)S(1)}, f32[2,16,1,1280]{3,1,2,0:T(8,128)S(1)}, u32[]{:S(2)}, u32[]{:S(2)}) collective-permute-start(f32[2,16,1,1280]{3,1,2,0:T(8,128)S(1)} %copy.32), channel_id=1, source_target_pairs={{1,0},{2,1},{3,2},{5,4},{6,5},{7,6},{9,8},{10,9},{11,10},{13,12},{... | collective-permute-start | bytes 491528 | tf_op jit(solution)/shard_map/ppermute | solution.py:19
  38.8 6.6 %collective-permute-start.7 = (f32[2,16,1,1280]{3,1,2,0:T(8,128)S(1)}, f32[2,16,1,1280]{3,1,2,0:T(8,128)S(1)}, u32[]{:S(2)}, u32[]{:S(2)}) collective-permute-start(f32[2,16,1,1280]{3,1,2,0:T(8,128)S(1)} %copy.34), channel_id=1, source_target_pairs={{0,1},{1,2},{2,3},{4,5},{5,6},{6,7},{8,9},{9,10},{10,11},{12,13},{... | collective-permute-start | bytes 491528 | tf_op jit(solution)/shard_map/ppermute | solution.py:17
  47.3 7.4 %collective-permute-start.8 = (f32[2,16,1,1280]{3,1,2,0:T(8,128)S(1)}, f32[2,16,1,1280]{3,1,2,0:T(8,128)S(1)}, u32[]{:S(2)}, u32[]{:S(2)}) collective-permute-start(f32[2,16,1,1280]{3,1,2,0:T(8,128)S(1)} %copy.36), channel_id=1, source_target_pairs={{1,0},{2,1},{3,2},{5,4},{6,5},{7,6},{9,8},{10,9},{11,10},{13,12},{... | collective-permute-start | bytes 491528 | tf_op jit(solution)/shard_map/ppermute | solution.py:19
  49.2 6.6 %collective-permute-start.9 = (f32[2,16,1,1280]{3,1,2,0:T(8,128)S(1)}, f32[2,16,1,1280]{3,1,2,0:T(8,128)S(1)}, u32[]{:S(2)}, u32[]{:S(2)}) collective-permute-start(f32[2,16,1,1280]{3,1,2,0:T(8,128)S(1)} %copy.38), channel_id=1, source_target_pairs={{0,1},{1,2},{2,3},{4,5},{5,6},{6,7},{8,9},{9,10},{10,11},{12,13},{... | collective-permute-start | bytes 491528 | tf_op jit(solution)/shard_map/ppermute | solution.py:17
  56.0 1.7 copy-start.1
  59.9 458.8 %all-gather.5.cloned.1.call-start = ((), (), s32[]{:S(2)}) async-start(), calls=%async_computation | async-start | bytes 2949120 | tf_op jit(solution)/shard_map/all_gather | solution.py:65
  60.6 513.3 %all-gather.7.cloned.1.call-start = ((), (), s32[]{:S(2)}) async-start(), calls=%async_computation.1 | async-start | bytes 2949120 | tf_op jit(solution)/shard_map/all_gather | solution.py:66
  573.9 4.0 copy-start.2
  579.3 8.2 %collective-permute-start.10 = (f32[2,16,1,1280]{3,1,2,0:T(8,128)S(1)}, f32[2,16,1,1280]{3,1,2,0:T(8,128)S(1)}, u32[]{:S(2)}, u32[]{:S(2)}) collective-permute-start(f32[2,16,1,1280]{3,1,2,0:T(8,128)S(1)} %copy.40), channel_id=1, source_target_pairs={{1,0},{2,1},{3,2},{5,4},{6,5},{7,6},{9,8},{10,9},{11,10},{13,12},{... | collective-permute-start | bytes 491528 | tf_op jit(solution)/shard_map/ppermute | solution.py:19
  583.5 5.2 collective-permute-start.11
  590.6 7.4 %collective-permute-start.12 = (f32[2,16,1,1280]{3,1,2,0:T(8,128)S(1)}, f32[2,16,1,1280]{3,1,2,0:T(8,128)S(1)}, u32[]{:S(2)}, u32[]{:S(2)}) collective-permute-start(f32[2,16,1,1280]{3,1,2,0:T(8,128)S(1)} %copy.44), channel_id=1, source_target_pairs={{1,0},{2,1},{3,2},{5,4},{6,5},{7,6},{9,8},{10,9},{11,10},{13,12},{... | collective-permute-start | bytes 491528 | tf_op jit(solution)/shard_map/ppermute | solution.py:19
  592.5 6.6 %collective-permute-start.13 = (f32[2,16,1,1280]{3,1,2,0:T(8,128)S(1)}, f32[2,16,1,1280]{3,1,2,0:T(8,128)S(1)}, u32[]{:S(2)}, u32[]{:S(2)}) collective-permute-start(f32[2,16,1,1280]{3,1,2,0:T(8,128)S(1)} %copy.46), channel_id=1, source_target_pairs={{0,1},{1,2},{2,3},{4,5},{5,6},{6,7},{8,9},{9,10},{10,11},{12,13},{... | collective-permute-start | bytes 491528 | tf_op jit(solution)/shard_map/ppermute | solution.py:17
  601.0 7.4 %collective-permute-start.14 = (f32[2,16,1,1280]{3,1,2,0:T(8,128)S(1)}, f32[2,16,1,1280]{3,1,2,0:T(8,128)S(1)}, u32[]{:S(2)}, u32[]{:S(2)}) collective-permute-start(f32[2,16,1,1280]{3,1,2,0:T(8,128)S(1)} %copy.48), channel_id=1, source_target_pairs={{1,0},{2,1},{3,2},{5,4},{6,5},{7,6},{9,8},{10,9},{11,10},{13,12},{... | collective-permute-start | bytes 491528 | tf_op jit(solution)/shard_map/ppermute | solution.py:19
  603.0 6.6 %collective-permute-start.15 = (f32[2,16,1,1280]{3,1,2,0:T(8,128)S(1)}, f32[2,16,1,1280]{3,1,2,0:T(8,128)S(1)}, u32[]{:S(2)}, u32[]{:S(2)}) collective-permute-start(f32[2,16,1,1280]{3,1,2,0:T(8,128)S(1)} %copy.50), channel_id=1, source_target_pairs={{0,1},{1,2},{2,3},{4,5},{5,6},{6,7},{8,9},{9,10},{10,11},{12,13},{... | collective-permute-start | bytes 491528 | tf_op jit(solution)/shard_map/ppermute | solution.py:17
  611.5 7.4 %collective-permute-start.16 = (f32[2,16,1,1280]{3,1,2,0:T(8,128)S(1)}, f32[2,16,1,1280]{3,1,2,0:T(8,128)S(1)}, u32[]{:S(2)}, u32[]{:S(2)}) collective-permute-start(f32[2,16,1,1280]{3,1,2,0:T(8,128)S(1)} %copy.52), channel_id=1, source_target_pairs={{1,0},{2,1},{3,2},{5,4},{6,5},{7,6},{9,8},{10,9},{11,10},{13,12},{... | collective-permute-start | bytes 491528 | tf_op jit(solution)/shard_map/ppermute | solution.py:19
  613.5 6.6 %collective-permute-start.17 = (f32[2,16,1,1280]{3,1,2,0:T(8,128)S(1)}, f32[2,16,1,1280]{3,1,2,0:T(8,128)S(1)}, u32[]{:S(2)}, u32[]{:S(2)}) collective-permute-start(f32[2,16,1,1280]{3,1,2,0:T(8,128)S(1)} %copy.54), channel_id=1, source_target_pairs={{0,1},{1,2},{2,3},{4,5},{5,6},{6,7},{8,9},{9,10},{10,11},{12,13},{... | collective-permute-start | bytes 491528 | tf_op jit(solution)/shard_map/ppermute | solution.py:17
Sparse Core Ops, SparseCore 0:
  60.0 403.4 all-gather.8
  465.7 52.9 all-gather.4
  520.9 52.9 all-gather.6
